TPU v7x, 32 devices: a whole 2x2x4 slice. The times are simulated.
32 devices in a mesh: dp: 4 (over x, core), row: 4 (over z), col: 2 (over y).
Axes of the slice: x: 2, y: 2, z: 4, core: 2. Of those that a mesh axis runs over, the one named last changes fastest.
Arguments:
- states: bfloat16 [8192, 2048], P(('dp', 'row'), 'col'), may hold values from -6 to 6
- keep: int32 [8192], P(('dp', 'row')), may hold values 0 or 1
- cont_ids: int32 [4, 1024], P('dp'), may hold values from 0 to 3, never falling along the last dimension, each value on 1 to 512 neighbouring positions
- answer_len: int32 [4, 4], P('dp'), may hold values from 1 to 512
- teacher: bfloat16 [8192, 2048], P(('dp', 'row'), 'col'), may hold values from -6 to 6
- out_grad: bfloat16 [8192, 2048], P(('dp', 'row'), 'col'), may hold values from -6 to 6
- gain_attn: float32 [2048], P('col'), may hold values from 0.5 to 1.5
- w_query: bfloat16 [2048, 2048], P('col', 'row'), may hold values from -0.125 to 0.125
- key_projection: bfloat16 [2048, 512], P('col', 'row'), may hold values from -0.125 to 0.125
- value_projection: bfloat16 [2048, 512], P('col', 'row'), may hold values from -0.125 to 0.125
- w_out: bfloat16 [2048, 2048], P('row', 'col'), may hold values from -1.5 to 1.5
- gain_ffn: float32 [2048], P('col'), may hold values from 0.5 to 1.5
- w_gate: bfloat16 [2048, 5632], P('col', 'row'), may hold values from -0.125 to 0.125
- w_up: bfloat16 [2048, 5632], P('col', 'row'), may hold values from -0.125 to 0.125
- w_down: bfloat16 [5632, 2048], P('row', 'col'), may hold values from -0.078125 to 0.078125
Outputs:
- output: bfloat16 [8192, 2048], P(('dp', 'row'), 'col')
- loss: float32 [], replicated
- grad_states: float32 [8192, 2048], P(('dp', 'row'), 'col')
- grad_gain_attn: float32 [2048], P('col')
- grad_query: float32 [2048, 2048], P('col', 'row')
- grad_key: float32 [2048, 512], P('col', 'row')
- grad_value: float32 [2048, 512], P('col', 'row')
- grad_out: float32 [2048, 2048], P('row', 'col')
- grad_gain_ffn: float32 [2048], P('col')
- grad_gate: float32 [2048, 5632], P('col', 'row')
- grad_up: float32 [2048, 5632], P('col', 'row')
- grad_down: float32 [5632, 2048], P('row', 'col')
Inputs may be any that keep to these rules, and one draw needn't show every extreme that they name: `cont_ids`: in each group the continuation numbers never fall along the tokens, and each continuation has 1 to 512 tokens.
All inputs are finite; a program needn't handle non-finite values. No bound on the sum of `keep` on one device may be relied on, other than what follows from the above.
Results may differ from a plain program's by a relative error of at most 0.019.
Values may be sent and summed in bfloat16 or wider, within the bound.
No kernel may reach another device: no remote copies, remote signals or barrier semaphores. Data moves between devices by JAX's collectives and lax.ppermute only.
A program may use at most 192 MiB of HBM per device.

v0:
```python
import jax
import jax.numpy as jnp
from jax import lax
from jax.sharding import PartitionSpec as P

MODEL_WIDTH = 2048
HEAD_SIZE = 128
PROMPT = 1024
EPSILON = 1e-05
MASKED = -1e30
ROPE_BASE = 10000.0


def rows_of(values, start, count, axis=0):
    return lax.dynamic_slice_in_dim(values, start, count, axis)


def token_layout(cont_ids, answer_len):
    groups, cont_tokens = cont_ids.shape
    labels = jnp.arange(answer_len.shape[1], dtype=jnp.int32)
    starts = jnp.sum((cont_ids[:, None, :] < labels[None, :, None]).astype(jnp.int32), axis=2)
    member = (cont_ids[:, :, None] == labels[None, None, :]).astype(jnp.int32)
    own_start = jnp.sum(member * starts[:, None, :], axis=2)
    own_limit = jnp.sum(member * answer_len[:, None, :], axis=2)
    offset = jnp.arange(cont_tokens, dtype=jnp.int32)[None, :] - own_start
    prompt_pos = jnp.arange(PROMPT, dtype=jnp.int32)[None, :]
    positions = jnp.concatenate([prompt_pos, PROMPT + offset], axis=1).reshape(-1)
    segment = jnp.concatenate(
        [jnp.full((groups, PROMPT), -1, dtype=jnp.int32), cont_ids], axis=1
    ).reshape(-1)
    counted = jnp.concatenate(
        [jnp.ones((groups, PROMPT), jnp.int32), (offset < own_limit).astype(jnp.int32)], axis=1
    ).reshape(-1)
    return (positions, segment, counted)


def rotary(values, positions, sign):
    half = values.shape[-1] // 2
    freqs = ROPE_BASE ** (-2.0 * jnp.arange(half, dtype=jnp.float32) / values.shape[-1])
    angles = positions.astype(jnp.float32)[:, None] * freqs[None, :]
    cosine = jnp.cos(angles)[:, None, :]
    sine = sign * jnp.sin(angles)[:, None, :]
    first = values[..., :half]
    second = values[..., half:]
    return jnp.concatenate(
        [first * cosine - second * sine, second * cosine + first * sine], axis=-1
    )


def visible(query_index, query_segment, key_index, key_segment):
    earlier = key_index[None, :] <= query_index[:, None]
    shared = (key_segment[None, :] < 0) | (key_segment[None, :] == query_segment[:, None])
    return earlier & shared


def feature_sum(values):
    return lax.psum(values, "col")


def gather_rows(values):
    return lax.all_gather(values, "row", axis=0, tiled=True)


def gather_cols(values):
    return lax.all_gather(values, "col", axis=0, tiled=True)


def partial_cols(term, count):
    return lax.psum_scatter(
        term(jnp.int32(0), count * lax.axis_size("col")), "col", scatter_dimension=0, tiled=True
    )


def partial_rows(term, count):
    return lax.psum_scatter(
        term(jnp.int32(0), count * lax.axis_size("row")), "row", scatter_dimension=0, tiled=True
    )


def body(
    states,
    keep,
    cont_ids,
    answer_len,
    teacher,
    out_grad,
    gain_attn,
    w_query,
    key_projection,
    value_projection,
    w_out,
    gain_ffn,
    w_gate,
    w_up,
    w_down,
):
    local_rows = states.shape[0]
    whole_rows = local_rows * lax.axis_size("row")
    query_rows = whole_rows // lax.axis_size("col")
    group_tokens = PROMPT + cont_ids.shape[1]
    key_heads = key_projection.shape[1] // HEAD_SIZE
    heads_per_group = w_query.shape[1] // key_projection.shape[1]
    query_width = w_query.shape[1]
    scale = HEAD_SIZE ** (-0.5)
    block = min(512, query_rows)
    blocks = query_rows // block
    positions, segment, counted = token_layout(cont_ids, answer_len)
    token_index = jnp.arange(whole_rows, dtype=jnp.int32)
    row_start = lax.axis_index("row") * local_rows
    col_start = lax.axis_index("col") * query_rows
    counted_here = rows_of(counted, row_start, local_rows).astype(jnp.float32)[:, None]
    query_pos = rows_of(positions, col_start, query_rows)
    keep_here = keep.astype(jnp.float32)[:, None]
    states_f = states.astype(jnp.float32)
    scale_attn = lax.rsqrt(
        feature_sum(jnp.sum(states_f * states_f, axis=1)) / MODEL_WIDTH + EPSILON
    )[:, None]
    normed_attn = (states_f * scale_attn * gain_attn[None, :]).astype(jnp.bfloat16)
    normed_all = gather_rows(normed_attn)
    w_kv = jnp.concatenate([key_projection, value_projection], axis=1)
    query_raw = partial_cols(
        lambda start, count: jnp.dot(
            rows_of(normed_all, start, count), w_query, preferred_element_type=jnp.float32
        ),
        query_rows,
    )
    kv_raw = lax.psum(jnp.dot(normed_all, w_kv, preferred_element_type=jnp.float32), "col")
    queries = (
        rotary(
            query_raw.reshape(query_rows, key_heads * heads_per_group, HEAD_SIZE), query_pos, 1.0
        )
        .astype(jnp.bfloat16)
        .reshape(query_rows, key_heads, heads_per_group, HEAD_SIZE)
    )
    keys = rotary(
        kv_raw[:, : key_heads * HEAD_SIZE].reshape(whole_rows, key_heads, HEAD_SIZE), positions, 1.0
    ).astype(jnp.bfloat16)
    values = (
        kv_raw[:, key_heads * HEAD_SIZE :]
        .reshape(whole_rows, key_heads, HEAD_SIZE)
        .astype(jnp.bfloat16)
    )

    def context_of(index):
        first = col_start + index * block
        key_first = first // group_tokens * group_tokens
        query_block = rows_of(queries, index * block, block)
        key_group = rows_of(keys, key_first, group_tokens)
        value_group = rows_of(values, key_first, group_tokens)
        raw = (
            jnp.einsum("qgjd,kgd->gjqk", query_block, key_group, preferred_element_type=jnp.float32)
            * scale
        )
        mask = visible(
            rows_of(token_index, first, block),
            rows_of(segment, first, block),
            rows_of(token_index, key_first, group_tokens),
            rows_of(segment, key_first, group_tokens),
        )
        scores = jnp.where(mask[None, None], raw, MASKED)
        return (query_block, key_group, value_group, scores, key_first)

    def attend(index):
        query_block, key_group, value_group, scores, key_first = context_of(index)
        peak = jnp.max(scores, axis=-1, keepdims=True)
        exponent = jnp.exp(scores - peak)
        totals = jnp.sum(exponent, axis=-1, keepdims=True)
        weights = (exponent / totals).astype(jnp.bfloat16)
        mixed = jnp.einsum(
            "gjqk,kgd->qgjd", weights, value_group, preferred_element_type=jnp.float32
        )
        return (mixed, peak + jnp.log(totals))

    mixed_blocks, log_totals = lax.map(attend, jnp.arange(blocks, dtype=jnp.int32))
    attn_context = mixed_blocks.reshape(query_rows, query_width).astype(jnp.bfloat16)
    context_all = gather_cols(attn_context)
    attention = partial_rows(
        lambda start, count: jnp.dot(
            rows_of(context_all, start, count), w_out, preferred_element_type=jnp.float32
        ),
        local_rows,
    )
    hidden_res = states_f + keep_here * attention
    scale_ffn = lax.rsqrt(
        feature_sum(jnp.sum(hidden_res * hidden_res, axis=1)) / MODEL_WIDTH + EPSILON
    )[:, None]
    normed_ffn = (hidden_res * scale_ffn * gain_ffn[None, :]).astype(jnp.bfloat16)
    ffn_all = gather_rows(normed_ffn)
    w_pair = jnp.concatenate([w_gate, w_up], axis=1)
    inner = w_gate.shape[1]
    gate_up = partial_cols(
        lambda start, count: jnp.dot(
            rows_of(ffn_all, start, count), w_pair, preferred_element_type=jnp.float32
        ),
        query_rows,
    )
    gate = gate_up[:, :inner]
    up_proj = gate_up[:, inner:]
    sigma = jax.nn.sigmoid(gate)
    swish = gate * sigma
    hidden = (swish * up_proj).astype(jnp.bfloat16)
    hidden_all = gather_cols(hidden)
    feed = partial_rows(
        lambda start, count: jnp.dot(
            rows_of(hidden_all, start, count), w_down, preferred_element_type=jnp.float32
        ),
        local_rows,
    )
    result = hidden_res + keep_here * feed
    error = result - teacher.astype(jnp.float32)
    own_count = jnp.where(lax.axis_index("col") == 0, jnp.sum(counted_here), 0.0)
    error_total, token_count_sum = lax.psum(
        (jnp.sum(counted_here * error * error), own_count), ("dp", "row", "col")
    )
    loss = error_total / (token_count_sum * MODEL_WIDTH)
    grad_result = (
        out_grad.astype(jnp.float32) + 2.0 / (token_count_sum * MODEL_WIDTH) * counted_here * error
    )
    grad_feed = (keep_here * grad_result).astype(jnp.bfloat16)
    grad_feed_all = gather_rows(grad_feed)
    grad_down = jnp.einsum(
        "tf,td->fd", hidden_all, grad_feed_all, preferred_element_type=jnp.float32
    )
    grad_hidden = partial_cols(
        lambda start, count: jnp.einsum(
            "td,fd->tf",
            rows_of(grad_feed_all, start, count),
            w_down,
            preferred_element_type=jnp.float32,
        ),
        query_rows,
    )
    grad_gate_in = grad_hidden * up_proj * sigma * (1.0 + gate * (1.0 - sigma))
    grad_up_in = grad_hidden * swish
    grad_pair = jnp.concatenate([grad_gate_in, grad_up_in], axis=1).astype(jnp.bfloat16)
    grad_pair_all = gather_cols(grad_pair)
    grad_w_pair = jnp.einsum(
        "td,tf->df", ffn_all, grad_pair_all, preferred_element_type=jnp.float32
    )
    grad_normed_ffn = partial_rows(
        lambda start, count: jnp.einsum(
            "tf,df->td",
            rows_of(grad_pair_all, start, count),
            w_pair,
            preferred_element_type=jnp.float32,
        ),
        local_rows,
    )
    grad_gain_ffn = jnp.sum(grad_normed_ffn * hidden_res * scale_ffn, axis=0)
    weighted_ffn = grad_normed_ffn * gain_ffn[None, :]
    inner_ffn = feature_sum(jnp.sum(weighted_ffn * hidden_res, axis=1))[:, None]
    grad_hidden_res = (
        grad_result + scale_ffn * weighted_ffn - hidden_res * scale_ffn**3 * inner_ffn / MODEL_WIDTH
    )
    grad_attention = (keep_here * grad_hidden_res).astype(jnp.bfloat16)
    grad_att_all = gather_rows(grad_attention)
    grad_out = jnp.einsum(
        "to,td->od", context_all, grad_att_all, preferred_element_type=jnp.float32
    )
    grad_context = partial_cols(
        lambda start, count: jnp.einsum(
            "td,od->to",
            rows_of(grad_att_all, start, count),
            w_out,
            preferred_element_type=jnp.float32,
        ),
        query_rows,
    )
    grad_context = grad_context.astype(jnp.bfloat16).reshape(
        query_rows, key_heads, heads_per_group, HEAD_SIZE
    )

    def attend_back(carry, item):
        index, log_total = item
        query_block, key_group, value_group, scores, key_first = context_of(index)
        grad_block = rows_of(grad_context, index * block, block)
        probs = jnp.exp(scores - log_total)
        grad_probs = jnp.einsum(
            "qgjd,kgd->gjqk", grad_block, value_group, preferred_element_type=jnp.float32
        )
        row_dot = jnp.sum(probs * grad_probs, axis=-1, keepdims=True)
        grad_scores = (probs * (grad_probs - row_dot)).astype(jnp.bfloat16)
        grad_query_block = (
            jnp.einsum("gjqk,kgd->qgjd", grad_scores, key_group, preferred_element_type=jnp.float32)
            * scale
        )
        grad_key_group = (
            jnp.einsum(
                "gjqk,qgjd->kgd", grad_scores, query_block, preferred_element_type=jnp.float32
            )
            * scale
        )
        grad_value_group = jnp.einsum(
            "gjqk,qgjd->kgd",
            probs.astype(jnp.bfloat16),
            grad_block,
            preferred_element_type=jnp.float32,
        )
        pair = jnp.concatenate([grad_key_group, grad_value_group], axis=1)
        updated = rows_of(carry, key_first, group_tokens) + pair
        return (updated, grad_query_block)

    start_carry = jnp.zeros((whole_rows, 2 * key_heads, HEAD_SIZE), jnp.float32)
    grad_kv_part, grad_query_blocks = lax.scan(
        attend_back, start_carry, (jnp.arange(blocks, dtype=jnp.int32), log_totals)
    )
    grad_kv_sum = (
        lax.psum(
            grad_kv_part.reshape(whole_rows, 2 * key_heads * HEAD_SIZE).astype(jnp.bfloat16), "col"
        )
        .astype(jnp.float32)
        .reshape(whole_rows, 2 * key_heads, HEAD_SIZE)
    )
    grad_keys = rotary(grad_kv_sum[:, :key_heads], positions, -1.0)
    grad_kv = (
        jnp.concatenate([grad_keys, grad_kv_sum[:, key_heads:]], axis=1)
        .reshape(whole_rows, 2 * key_heads * HEAD_SIZE)
        .astype(jnp.bfloat16)
    )
    grad_queries = (
        rotary(
            grad_query_blocks.reshape(query_rows, key_heads * heads_per_group, HEAD_SIZE),
            query_pos,
            -1.0,
        )
        .reshape(query_rows, query_width)
        .astype(jnp.bfloat16)
    )
    grad_queries_all = gather_cols(grad_queries)
    grad_query = jnp.einsum(
        "td,tq->dq", normed_all, grad_queries_all, preferred_element_type=jnp.float32
    )
    grad_kv_weight = jnp.einsum(
        "td,tk->dk", normed_all, grad_kv, preferred_element_type=jnp.float32
    )
    grad_key = grad_kv_weight[:, : key_heads * HEAD_SIZE]
    grad_value = grad_kv_weight[:, key_heads * HEAD_SIZE :]

    def back_terms(start, count):
        from_queries = jnp.einsum(
            "tq,dq->td",
            rows_of(grad_queries_all, start, count),
            w_query,
            preferred_element_type=jnp.float32,
        )
        from_kv = jnp.einsum(
            "tk,dk->td", rows_of(grad_kv, start, count), w_kv, preferred_element_type=jnp.float32
        )
        return from_queries + from_kv

    grad_normed_attn = partial_rows(back_terms, local_rows)
    grad_gain_attn = jnp.sum(grad_normed_attn * states_f * scale_attn, axis=0)
    weighted_attn = grad_normed_attn * gain_attn[None, :]
    inner_attn = feature_sum(jnp.sum(weighted_attn * states_f, axis=1))[:, None]
    grad_states = (
        grad_hidden_res
        + scale_attn * weighted_attn
        - states_f * scale_attn**3 * inner_attn / MODEL_WIDTH
    )
    gain_attn_sum, gain_ffn_sum = lax.psum((grad_gain_attn, grad_gain_ffn), ("dp", "row"))
    summed = (
        lax.psum(grad_query.astype(jnp.bfloat16), "dp").astype(jnp.float32),
        lax.psum(grad_key.astype(jnp.bfloat16), "dp").astype(jnp.float32),
        lax.psum(grad_value.astype(jnp.bfloat16), "dp").astype(jnp.float32),
        lax.psum(grad_out.astype(jnp.bfloat16), "dp").astype(jnp.float32),
        lax.psum(grad_w_pair[:, :inner].astype(jnp.bfloat16), "dp").astype(jnp.float32),
        lax.psum(grad_w_pair[:, inner:].astype(jnp.bfloat16), "dp").astype(jnp.float32),
        lax.psum(grad_down.astype(jnp.bfloat16), "dp").astype(jnp.float32),
    )
    return (
        result.astype(jnp.bfloat16),
        loss,
        grad_states,
        gain_attn_sum,
        summed[0],
        summed[1],
        summed[2],
        summed[3],
        gain_ffn_sum,
        summed[4],
        summed[5],
        summed[6],
    )


def solution(mesh):
    return jax.shard_map(
        body,
        mesh=mesh,
        in_specs=(
            P(("dp", "row"), "col"),
            P(("dp", "row")),
            P("dp", None),
            P("dp", None),
            P(("dp", "row"), "col"),
            P(("dp", "row"), "col"),
            P("col"),
            P("col", "row"),
            P("col", "row"),
            P("col", "row"),
            P("row", "col"),
            P("col"),
            P("col", "row"),
            P("col", "row"),
            P("row", "col"),
        ),
        out_specs=(
            P(("dp", "row"), "col"),
            P(),
            P(("dp", "row"), "col"),
            P("col"),
            P("col", "row"),
            P("col", "row"),
            P("col", "row"),
            P("row", "col"),
            P("col"),
            P("col", "row"),
            P("col", "row"),
            P("row", "col"),
        ),
        check_vma=False,
    )
```

profile of v0, /device:TPU:0, one launch (start us, length us, event | category | flops | bytes accessed | tf_op | source)
XLA Modules:
  0.0 2396.0 jit_solution(15382242776699901373)
XLA Ops:
  20.5 80.6 %all-gather.9.cloned.1.call-done = bf16[2048,1024]{1,0:T(8,128)(2,1)} async-done(((bf16[512,1024]{1,0:T(8,128)(2,1)}), bf16[2048,1024]{1,0:T(8,128)(2,1)}) %all-gather.9.cloned.1.call-update) | async-done | bytes 4194320 | tf_op jit(solution)/shard_map/all_gather | solution.py:61
  118.2 49.4 %all-reduce.9.cloned.1.call-done = f32[2048,256]{0,1:T(8,128)} async-done(((f32[2048,256]{0,1:T(8,128)}), f32[2048,256]{0,1:T(8,128)}) %all-reduce.9.cloned.1.call-update) | async-done | bytes 2097168 | tf_op jit(solution)/shard_map/psum | solution.py:127
  177.6 47.3 %reduce-scatter.9.cloned.1.call-done = f32[1024,512]{1,0:T(8,128)} async-done(((f32[2048,512]{1,0:T(8,128)}), f32[1024,512]{1,0:T(8,128)}) %reduce-scatter.9.cloned.1.call-update) | async-done | bytes 2097168 | tf_op jit(solution)/shard_map/reduce_scatter | solution.py:69
  233.5 36.7 %while.27 = (s32[]{:T(128)}, bf16[2,512,1,4,128]{4,1,3,2,0:T(8,128)(2,1)}, f32[2,1,4,512,1]{3,2,4,1,0:T(4,128)S(1)}, s32[2048]{0:T(1024)S(1)}, s32[2]{0:T(128)S(...) while((s32[]{:T(128)}, ...), condition=%wide.region_9.10_spmd.clone, body=%wide.region_6.9_spmd.clone.sunk | while | flops 2202009600 | bytes 65642824 | solution.py:174
  273.8 32.8 %all-gather.11.cloned.1.call-done = bf16[2048,512]{1,0:T(8,128)(2,1)} async-done(((bf16[1024,512]{1,0:T(8,128)(2,1)}), bf16[2048,512]{1,0:T(8,128)(2,1)}) %all-gather.11.cloned.1.call-update) | async-done | bytes 2097168 | tf_op jit(solution)/shard_map/all_gather | solution.py:65
  314.8 144.0 %reduce-scatter.11.cloned.1.call-done = f32[512,1024]{1,0:T(8,128)} async-done(((f32[2048,1024]{1,0:T(8,128)}), f32[512,1024]{1,0:T(8,128)}) %reduce-scatter.11.cloned.1.call-update) | async-done | bytes 2097168 | tf_op jit(solution)/shard_map/reduce_scatter | solution.py:75
  475.8 76.0 %all-gather.13.cloned.1.call-done = bf16[2048,1024]{1,0:T(8,128)(2,1)} async-done(((bf16[512,1024]{1,0:T(8,128)(2,1)}), bf16[2048,1024]{1,0:T(8,128)(2,1)}) %all-gather.13.cloned.1.call-update) | async-done | bytes 4194320 | tf_op jit(solution)/shard_map/all_gather | solution.py:61
  551.8 19.7 fusion.94
  571.6 255.4 %reduce-scatter.13.cloned.1.call-done = f32[1024,2816]{1,0:T(8,128)} async-done(((f32[2048,2816]{1,0:T(8,128)}), f32[1024,2816]{1,0:T(8,128)}) %reduce-scatter.13.cloned.1.call-update) | async-done | bytes 11534352 | tf_op jit(solution)/shard_map/reduce_scatter | solution.py:69
  833.3 74.6 %all-gather.15.cloned.1.call-done = bf16[2048,1408]{1,0:T(8,128)(2,1)} async-done(((bf16[1024,1408]{1,0:T(8,128)(2,1)}), bf16[2048,1408]{1,0:T(8,128)(2,1)}) %all-gather.15.cloned.1.call-update) | async-done | bytes 5767184 | tf_op jit(solution)/shard_map/all_gather | solution.py:65
  920.6 142.7 %reduce-scatter.15.cloned.1.call-done = f32[512,1024]{1,0:T(8,128)} async-done(((f32[2048,1024]{1,0:T(8,128)}), f32[512,1024]{1,0:T(8,128)}) %reduce-scatter.15.cloned.1.call-update) | async-done | bytes 2097168 | tf_op jit(solution)/shard_map/reduce_scatter | solution.py:75
  1068.3 41.1 %all-reduce.2 = (f32[]{:T(128)}, f32[]{:T(128)}) all-reduce(f32[]{:T(128)} %get-tuple-element.352, f32[]{:T(128)S(6)} %select_n.47), channel_id=1, replica_groups=mesh['dp'=4,'row'=4,'col'=2] {'dp','row','col'}, use_global_device_ids=true, to_apply=%region_17.18 | all-reduce | flops 2 | bytes 16 | tf_op jit(solution)/shard_map/psum | solution.py:212
  1113.8 80.8 %all-gather.17.cloned.1.call-done = bf16[2048,1024]{1,0:T(8,128)(2,1)} async-done(((bf16[512,1024]{1,0:T(8,128)(2,1)}), bf16[2048,1024]{1,0:T(8,128)(2,1)}) %all-gather.17.cloned.1.call-update) | async-done | bytes 4194320 | tf_op jit(solution)/shard_map/all_gather | solution.py:61
  1205.9 131.8 %reduce-scatter.17.cloned.1.call-done = f32[1024,1408]{1,0:T(8,128)} async-done(((f32[2048,1408]{1,0:T(8,128)}), f32[1024,1408]{1,0:T(8,128)}) %reduce-scatter.17.cloned.1.call-update) | async-done | bytes 5767184 | tf_op jit(solution)/shard_map/reduce_scatter | solution.py:69
  1348.1 141.1 %all-gather.19.cloned.1.call-done = bf16[2048,2816]{1,0:T(8,128)(2,1)} async-done(((bf16[1024,2816]{1,0:T(8,128)(2,1)}), bf16[2048,2816]{1,0:T(8,128)(2,1)}) %all-gather.19.cloned.1.call-update) | async-done | bytes 11534352 | tf_op jit(solution)/shard_map/all_gather | solution.py:65
  1507.3 144.6 %reduce-scatter.19.cloned.1.call-done = f32[512,1024]{1,0:T(8,128)} async-done(((f32[2048,1024]{1,0:T(8,128)}), f32[512,1024]{1,0:T(8,128)}) %reduce-scatter.19.cloned.1.call-update) | async-done | bytes 2097168 | tf_op jit(solution)/shard_map/reduce_scatter | solution.py:75
  1665.1 81.6 %all-gather.21.cloned.1.call-done = bf16[2048,1024]{1,0:T(8,128)(2,1)} async-done(((bf16[512,1024]{1,0:T(8,128)(2,1)}), bf16[2048,1024]{1,0:T(8,128)(2,1)}) %all-gather.21.cloned.1.call-update) | async-done | bytes 4194320 | tf_op jit(solution)/shard_map/all_gather | solution.py:61
  1764.5 42.0 %reduce-scatter.21.cloned.1.call-done = f32[1024,512]{1,0:T(8,128)} async-done(((f32[2048,512]{1,0:T(8,128)}), f32[1024,512]{1,0:T(8,128)}) %reduce-scatter.21.cloned.1.call-update) | async-done | bytes 2097168 | tf_op jit(solution)/shard_map/reduce_scatter | solution.py:69
  1809.4 100.4 %while.28 = (s32[]{:T(128)}, f32[2048,2,128]{0,2,1:T(8,128)}, f32[2,512,1,4,128]{4,1,0,3,2:T(8,128)}, s32[2]{0:T(128)S(1)}, bf16[1024,1,4,128]{3,0,2,1:T(8,128)(...) while((s32[]{:T(128)}, f32[2048,2,128]{0,2,1:T(8,128)}, ...), condition=%wide.region_27.28_spmd.clone.clone, body=%wide.region_25.27_spmd.clone.clone.sunk | while | flops 5437915136 | bytes 244941232 | solution.py:304
  1912.6 19.1 convolution_convert_fusion
  1959.2 28.7 %all-gather.23.cloned.1.call-done = bf16[2048,512]{0,1:T(8,128)(2,1)} async-done(((bf16[1024,512]{0,1:T(8,128)(2,1)}), bf16[2048,512]{0,1:T(8,128)(2,1)}) %all-gather.23.cloned.1.call-update) | async-done | bytes 2097168 | tf_op jit(solution)/shard_map/all_gather | solution.py:65
  2004.7 191.2 %all-reduce.13.cloned.1.call-done = (bf16[1024,512]{1,0:T(8,128)(2,1)}, bf16[1024,128]{1,0:T(8,128)(2,1)}, bf16[1024,128]{1,0:T(8,128)(2,1)}, bf16[512,1024]{1,0...) async-done(((bf16[1024,512]{1,0:T(8,128)(2,1)}, bf16[1024,128]{1,0:T(8,128)(2,1)}, bf16[1024,128]{1,0:T(8,128)(2,1)}, ...) | async-done | bytes 11272208 | tf_op jit(solution)/shard_map/psum | solution.py:362
  2214.1 128.9 %reduce-scatter.23.cloned.1.call-done = f32[512,1024]{1,0:T(8,128)} async-done(((f32[2048,1024]{1,0:T(8,128)}), f32[512,1024]{1,0:T(8,128)}) %reduce-scatter.23.cloned.1.call-update) | async-done | bytes 2097168 | tf_op jit(solution)/shard_map/reduce_scatter | solution.py:75
  2350.2 33.3 %all-reduce.3 = (f32[1024]{0:T(1024)}, f32[1024]{0:T(1024)}) all-reduce(f32[1024]{0:T(1024)S(1)} %get-tuple-element.289, f32[1024]{0:T(1024)S(1)} %copy-done.33), channel_id=1, replica_groups=mesh['dp'=4,'row'=4,'col'=2] {'dp','row'}, use_global_device_ids=true, to_apply=%region_33.34 | all-reduce | flops 2048 | bytes 16384 | tf_op jit(solution)/shard_map/psum | solution.py:360
  (276 shorter events, 388.0 us)
Async XLA Ops:
  7.2 900.8 %copy-start = (bf16[1408,1024]{1,0:T(8,128)(2,1)S(1)}, bf16[1408,1024]{1,0:T(8,128)(2,1)}, u32[]{:S(2)}) copy-start(bf16[1408,1024]{1,0:T(8,128)(2,1)} %param.33) | copy-start | bytes 8650756
  7.2 94.0 %all-gather.9.cloned.1.call-start = ((), (), s32[]{:S(2)}) async-start(), calls=%async_computation.8 | async-start | bytes 5242880 | tf_op jit(solution)/shard_map/all_gather | solution.py:61
  18.5 149.1 %all-reduce.9.cloned.1.call-start = ((), (), s32[]{:S(2)}) async-start(), calls=%async_computation.10 | async-start | bytes 4194304 | tf_op jit(solution)/shard_map/psum | solution.py:127
  106.0 118.9 %reduce-scatter.9.cloned.1.call-start = ((), (), s32[]{:S(2)}) async-start(), calls=%async_computation.9 | async-start | bytes 6291456 | tf_op jit(solution)/shard_map/reduce_scatter | solution.py:69
  112.9 193.8 %all-gather.11.cloned.1.call-start = ((), (), s32[]{:S(2)}) async-start(), calls=%async_computation.11 | async-start | bytes 3145728 | tf_op jit(solution)/shard_map/all_gather | solution.py:65
  273.4 185.4 %reduce-scatter.11.cloned.1.call-start = ((), (), s32[]{:S(2)}) async-start(), calls=%async_computation.12 | async-start | bytes 10485760 | tf_op jit(solution)/shard_map/reduce_scatter | solution.py:75
  314.2 153.1 %copy-start.27 = (f32[1024]{0:T(1024)S(1)}, f32[1024]{0:T(1024)}, u32[]{:S(2)}) copy-start(f32[1024]{0:T(1024)} %param.30) | copy-start | bytes 12292
  314.2 237.6 %all-gather.13.cloned.1.call-start = ((), (), s32[]{:S(2)}) async-start(), calls=%async_computation.13 | async-start | bytes 5242880 | tf_op jit(solution)/shard_map/all_gather | solution.py:61
  470.2 356.8 %reduce-scatter.13.cloned.1.call-start = ((), (), s32[]{:S(2)}) async-start(), calls=%async_computation.14 | async-start | bytes 34603008 | tf_op jit(solution)/shard_map/reduce_scatter | solution.py:69
  571.6 336.4 %all-gather.15.cloned.1.call-start = ((), (), s32[]{:S(2)}) async-start(), calls=%async_computation.15 | async-start | bytes 8650752 | tf_op jit(solution)/shard_map/all_gather | solution.py:65
  833.3 230.0 %reduce-scatter.15.cloned.1.call-start = ((), (), s32[]{:S(2)}) async-start(), calls=%async_computation.16 | async-start | bytes 10485760 | tf_op jit(solution)/shard_map/reduce_scatter | solution.py:75
  918.6 276.0 %all-gather.17.cloned.1.call-start = ((), (), s32[]{:S(2)}) async-start(), calls=%async_computation.17 | async-start | bytes 5242880 | tf_op jit(solution)/shard_map/all_gather | solution.py:61
  1113.8 223.9 %reduce-scatter.17.cloned.1.call-start = ((), (), s32[]{:S(2)}) async-start(), calls=%async_computation.18 | async-start | bytes 17301504 | tf_op jit(solution)/shard_map/reduce_scatter | solution.py:69
  1205.8 283.3 %all-gather.19.cloned.1.call-start = ((), (), s32[]{:S(2)}) async-start(), calls=%async_computation.19 | async-start | bytes 17301504 | tf_op jit(solution)/shard_map/all_gather | solution.py:65
  1348.0 303.8 %reduce-scatter.19.cloned.1.call-start = ((), (), s32[]{:S(2)}) async-start(), calls=%async_computation.20 | async-start | bytes 10485760 | tf_op jit(solution)/shard_map/reduce_scatter | solution.py:75
  1507.2 144.7 %copy-start.5 = (f32[512,1024]{1,0:T(8,128)S(1)}, f32[512,1024]{1,0:T(8,128)}, u32[]{:S(2)}) copy-start(f32[512,1024]{1,0:T(8,128)} %get-tuple-element.355) | copy-start | bytes 6291460
  1507.2 239.5 %all-gather.21.cloned.1.call-start = ((), (), s32[]{:S(2)}) async-start(), calls=%async_computation.21 | async-start | bytes 5242880 | tf_op jit(solution)/shard_map/all_gather | solution.py:61
  1665.0 141.5 %reduce-scatter.21.cloned.1.call-start = ((), (), s32[]{:S(2)}) async-start(), calls=%async_computation.22 | async-start | bytes 6291456 | tf_op jit(solution)/shard_map/reduce_scatter | solution.py:69
  1753.6 199.1 %all-reduce.11.cloned.1.call-start = ((), (), s32[]{:S(2)}) async-start(), calls=%async_computation.24 | async-start | bytes 2097152 | tf_op jit(solution)/shard_map/psum | solution.py:308
  1912.6 75.3 %all-gather.23.cloned.1.call-start = ((), (), s32[]{:S(2)}) async-start(), calls=%async_computation.23 | async-start | bytes 3145728 | tf_op jit(solution)/shard_map/all_gather | solution.py:65
  1934.4 261.5 %all-reduce.13.cloned.1.call-start = ((), (), s32[]{:S(2)}) async-start(), calls=%async_computation.26 | async-start | bytes 22544384 | tf_op jit(solution)/shard_map/psum | solution.py:362
  1994.1 348.8 %reduce-scatter.23.cloned.1.call-start = ((), (), s32[]{:S(2)}) async-start(), calls=%async_computation.25 | async-start | bytes 10485760 | tf_op jit(solution)/shard_map/reduce_scatter | solution.py:75
  2214.1 136.1 %copy-start.33 = (f32[1024]{0:T(1024)S(1)}, f32[1024]{0:T(1024)}, u32[]{:S(2)}) copy-start(f32[1024]{0:T(1024)} %get-tuple-element.287) | copy-start | bytes 12292
  2214.1 169.4 %copy-start.35 = (f32[512]{0:T(512)S(1)}, f32[512]{0:T(512)}, u32[]{:S(2)}) copy-start(f32[512]{0:T(512)} %get-tuple-element.380) | copy-start | bytes 6148
  (47 other events, 824.1 us)
Sparse Core Ops, SparseCore 0:
  18.6 82.5 all-gather.8
  106.1 61.4 all-reduce.8
  170.6 54.3 reduce-scatter.8
  273.5 33.1 all-gather.10
  314.3 144.4 reduce-scatter.10
  470.3 81.4 all-gather.12
  571.7 255.2 reduce-scatter.12
  833.4 74.4 all-gather.14
  918.8 144.4 reduce-scatter.14
  1113.9 80.7 all-gather.16
  1206.0 131.6 reduce-scatter.16
  1348.1 141.0 all-gather.18
  1507.3 144.4 reduce-scatter.18
  1665.2 81.4 all-gather.20
  1753.7 52.8 reduce-scatter.20
  1912.7 40.0 all-reduce.10
  1954.7 33.1 all-gather.22
  1994.2 201.6 all-reduce.12
  2198.2 144.6 reduce-scatter.22
where the time goes:
time: 2400 us
  waiting for transfers between devices  1880 us (78%)
  matrix products  207 us (9%)
  other arithmetic  128 us (5%)
  blocking collectives  95.1 us (4%)
  local copies, waits for them, and re-layouts  60.3 us (3%)
    reduce_scatter x4, waiting for transfers between devices, partial_rows(): lax.psum_scatter(term(jnp.int32(0), count * lax.axis_size('row')), 'row',...  560 us
    reduce_scatter x4, waiting for transfers between devices, partial_cols(): lax.psum_scatter(term(jnp.int32(0), count * lax.axis_size('col')), 'col',...  477 us
    all_gather x4, waiting for transfers between devices, gather_rows(): return lax.all_gather(values, 'row', axis=0, tiled=True)  319 us
    all_gather x4, waiting for transfers between devices, gather_cols(): return lax.all_gather(values, 'col', axis=0, tiled=True)  277 us
    psum x1, waiting for transfers between devices, body(): lax.psum(grad_query.astype(jnp.bfloat16), 'dp').astype(jnp.float32)  191 us
    psum x1, waiting for transfers between devices, body(): lax.psum(jnp.dot(normed_all, w_kv, preferred_element_type=jnp.float32), '...  49.4 us
  transfers between devices with their start and end apart: 19, of which 19 were waited for; matrix products, arithmetic and copies ran while one was open for 4% of the time, Pallas kernels for 0%

commit v1 on v0

--- a/solution.py
+++ b/solution.py
@@ -124,7 +124,8 @@
         ),
         query_rows,
     )
-    kv_raw = lax.psum(jnp.dot(normed_all, w_kv, preferred_element_type=jnp.float32), "col")
+    page = jnp.dot(normed_all, w_kv, preferred_element_type=jnp.float32)
+    kv_raw = jax.lax.all_gather(page, "col").sum(axis=0)
     queries = (
         rotary(
             query_raw.reshape(query_rows, key_heads * heads_per_group, HEAD_SIZE), query_pos, 1.0

time: 2400 us -> 2400 us (level)
    psum x1 -> x0, waiting for transfers between devices: 49.4 us -> none  [body(): lax.psum(jnp.dot(normed_all, w_kv, preferred_element_type=jnp.float32), '...]
    all_gather x0 -> x1, waiting for transfers between devices: none -> 43 us  [body(): kv_raw = jax.lax.all_gather(page, 'col').sum(axis=0)]
  transfers between devices with their start and end apart: 19 -> 19, of which waited for: 19 -> 19; matrix products, arithmetic and copies ran while one was open for 4% -> 5% of each run, Pallas kernels for 0% -> 0%
where the time goes in v1:
time: 2400 us; the launch traced here: 2390 us
  waiting for transfers between devices  1870 us (78%)
  matrix products  207 us (9%)
  other arithmetic  133 us (6%)
  blocking collectives  95.2 us (4%)
  local copies, waits for them, and re-layouts  60.7 us (3%)
    reduce_scatter x4, waiting for transfers between devices, partial_rows(): lax.psum_scatter(term(jnp.int32(0), count * lax.axis_size('row')), 'row',...  560 us
    reduce_scatter x4, waiting for transfers between devices, partial_cols(): lax.psum_scatter(term(jnp.int32(0), count * lax.axis_size('col')), 'col',...  471 us
    all_gather x4, waiting for transfers between devices, gather_rows(): return lax.all_gather(values, 'row', axis=0, tiled=True)  319 us
    all_gather x4, waiting for transfers between devices, gather_cols(): return lax.all_gather(values, 'col', axis=0, tiled=True)  277 us
    psum x1, waiting for transfers between devices, body(): lax.psum(grad_query.astype(jnp.bfloat16), 'dp').astype(jnp.float32)  191 us
  transfers between devices with their start and end apart: 19, of which 19 were waited for; matrix products, arithmetic and copies ran while one was open for 5% of the time, Pallas kernels for 0%

profile of v1, /device:TPU:0, one launch (start us, length us, event | category | flops | bytes accessed | tf_op | source)
XLA Modules:
  0.0 2390.0 jit_solution(15715515158893792449)
XLA Ops:
  20.5 80.6 %all-gather.11.cloned.1.call-done = bf16[2048,1024]{1,0:T(8,128)(2,1)} async-done(((bf16[512,1024]{1,0:T(8,128)(2,1)}), bf16[2048,1024]{1,0:T(8,128)(2,1)}) %all-gather.11.cloned.1.call-update) | async-done | bytes 4194320 | tf_op jit(solution)/shard_map/all_gather | solution.py:61
  118.4 43.0 %all-gather.27.cloned.1.call-done = f32[4096,256]{1,0:T(8,128)} async-done(((f32[2048,256]{1,0:T(8,128)}), f32[4096,256]{1,0:T(8,128)}) %all-gather.27.cloned.1.call-update) | async-done | bytes 4194320 | tf_op jit(solution)/shard_map/all_gather | solution.py:128
  176.3 42.3 %reduce-scatter.9.cloned.1.call-done = f32[1024,512]{1,0:T(8,128)} async-done(((f32[2048,512]{1,0:T(8,128)}), f32[1024,512]{1,0:T(8,128)}) %reduce-scatter.9.cloned.1.call-update) | async-done | bytes 2097168 | tf_op jit(solution)/shard_map/reduce_scatter | solution.py:69
  227.1 36.7 %while.27 = (s32[]{:T(128)}, bf16[2,512,1,4,128]{4,1,3,2,0:T(8,128)(2,1)}, f32[2,1,4,512,1]{3,2,4,1,0:T(4,128)S(1)}, s32[2048]{0:T(1024)S(1)}, s32[2]{0:T(128)S(...) while((s32[]{:T(128)}, ...), condition=%wide.region_9.10_spmd.clone, body=%wide.region_6.9_spmd.clone.sunk | while | flops 2202009600 | bytes 65642824 | solution.py:175
  267.5 32.8 %all-gather.13.cloned.1.call-done = bf16[2048,512]{1,0:T(8,128)(2,1)} async-done(((bf16[1024,512]{1,0:T(8,128)(2,1)}), bf16[2048,512]{1,0:T(8,128)(2,1)}) %all-gather.13.cloned.1.call-update) | async-done | bytes 2097168 | tf_op jit(solution)/shard_map/all_gather | solution.py:65
  308.5 144.0 %reduce-scatter.11.cloned.1.call-done = f32[512,1024]{1,0:T(8,128)} async-done(((f32[2048,1024]{1,0:T(8,128)}), f32[512,1024]{1,0:T(8,128)}) %reduce-scatter.11.cloned.1.call-update) | async-done | bytes 2097168 | tf_op jit(solution)/shard_map/reduce_scatter | solution.py:75
  469.4 76.1 %all-gather.15.cloned.1.call-done = bf16[2048,1024]{1,0:T(8,128)(2,1)} async-done(((bf16[512,1024]{1,0:T(8,128)(2,1)}), bf16[2048,1024]{1,0:T(8,128)(2,1)}) %all-gather.15.cloned.1.call-update) | async-done | bytes 4194320 | tf_op jit(solution)/shard_map/all_gather | solution.py:61
  545.5 19.7 fusion.94
  565.3 255.4 %reduce-scatter.13.cloned.1.call-done = f32[1024,2816]{1,0:T(8,128)} async-done(((f32[2048,2816]{1,0:T(8,128)}), f32[1024,2816]{1,0:T(8,128)}) %reduce-scatter.13.cloned.1.call-update) | async-done | bytes 11534352 | tf_op jit(solution)/shard_map/reduce_scatter | solution.py:69
  827.0 74.6 %all-gather.17.cloned.1.call-done = bf16[2048,1408]{1,0:T(8,128)(2,1)} async-done(((bf16[1024,1408]{1,0:T(8,128)(2,1)}), bf16[2048,1408]{1,0:T(8,128)(2,1)}) %all-gather.17.cloned.1.call-update) | async-done | bytes 5767184 | tf_op jit(solution)/shard_map/all_gather | solution.py:65
  914.3 142.7 %reduce-scatter.15.cloned.1.call-done = f32[512,1024]{1,0:T(8,128)} async-done(((f32[2048,1024]{1,0:T(8,128)}), f32[512,1024]{1,0:T(8,128)}) %reduce-scatter.15.cloned.1.call-update) | async-done | bytes 2097168 | tf_op jit(solution)/shard_map/reduce_scatter | solution.py:75
  1061.9 41.2 %all-reduce.2 = (f32[]{:T(128)}, f32[]{:T(128)}) all-reduce(f32[]{:T(128)} %get-tuple-element.396, f32[]{:T(128)S(6)} %select_n.47), channel_id=1, replica_groups=mesh['dp'=4,'row'=4,'col'=2] {'dp','row','col'}, use_global_device_ids=true, to_apply=%region_17.18 | all-reduce | flops 2 | bytes 16 | tf_op jit(solution)/shard_map/psum | solution.py:213
  1107.5 80.8 %all-gather.19.cloned.1.call-done = bf16[2048,1024]{1,0:T(8,128)(2,1)} async-done(((bf16[512,1024]{1,0:T(8,128)(2,1)}), bf16[2048,1024]{1,0:T(8,128)(2,1)}) %all-gather.19.cloned.1.call-update) | async-done | bytes 4194320 | tf_op jit(solution)/shard_map/all_gather | solution.py:61
  1199.6 131.8 %reduce-scatter.17.cloned.1.call-done = f32[1024,1408]{1,0:T(8,128)} async-done(((f32[2048,1408]{1,0:T(8,128)}), f32[1024,1408]{1,0:T(8,128)}) %reduce-scatter.17.cloned.1.call-update) | async-done | bytes 5767184 | tf_op jit(solution)/shard_map/reduce_scatter | solution.py:69
  1341.8 141.1 %all-gather.21.cloned.1.call-done = bf16[2048,2816]{1,0:T(8,128)(2,1)} async-done(((bf16[1024,2816]{1,0:T(8,128)(2,1)}), bf16[2048,2816]{1,0:T(8,128)(2,1)}) %all-gather.21.cloned.1.call-update) | async-done | bytes 11534352 | tf_op jit(solution)/shard_map/all_gather | solution.py:65
  1501.0 144.6 %reduce-scatter.19.cloned.1.call-done = f32[512,1024]{1,0:T(8,128)} async-done(((f32[2048,1024]{1,0:T(8,128)}), f32[512,1024]{1,0:T(8,128)}) %reduce-scatter.19.cloned.1.call-update) | async-done | bytes 2097168 | tf_op jit(solution)/shard_map/reduce_scatter | solution.py:75
  1658.8 81.6 %all-gather.23.cloned.1.call-done = bf16[2048,1024]{1,0:T(8,128)(2,1)} async-done(((bf16[512,1024]{1,0:T(8,128)(2,1)}), bf16[2048,1024]{1,0:T(8,128)(2,1)}) %all-gather.23.cloned.1.call-update) | async-done | bytes 4194320 | tf_op jit(solution)/shard_map/all_gather | solution.py:61
  1758.3 42.0 %reduce-scatter.21.cloned.1.call-done = f32[1024,512]{1,0:T(8,128)} async-done(((f32[2048,512]{1,0:T(8,128)}), f32[1024,512]{1,0:T(8,128)}) %reduce-scatter.21.cloned.1.call-update) | async-done | bytes 2097168 | tf_op jit(solution)/shard_map/reduce_scatter | solution.py:69
  1803.1 100.3 %while.28 = (s32[]{:T(128)}, f32[2048,2,128]{0,2,1:T(8,128)}, f32[2,512,1,4,128]{4,1,0,3,2:T(8,128)}, s32[2]{0:T(128)S(1)}, bf16[1024,1,4,128]{3,0,2,1:T(8,128)(...) while((s32[]{:T(128)}, f32[2048,2,128]{0,2,1:T(8,128)}, ...), condition=%wide.region_27.28_spmd.clone.clone, body=%wide.region_25.27_spmd.clone.clone.sunk | while | flops 5437915136 | bytes 244941232 | solution.py:305
  1906.3 19.1 convolution_convert_fusion
  1952.9 28.7 %all-gather.25.cloned.1.call-done = bf16[2048,512]{0,1:T(8,128)(2,1)} async-done(((bf16[1024,512]{0,1:T(8,128)(2,1)}), bf16[2048,512]{0,1:T(8,128)(2,1)}) %all-gather.25.cloned.1.call-update) | async-done | bytes 2097168 | tf_op jit(solution)/shard_map/all_gather | solution.py:65
  1998.5 191.2 %all-reduce.10.cloned.1.call-done = (bf16[1024,512]{1,0:T(8,128)(2,1)}, bf16[1024,128]{1,0:T(8,128)(2,1)}, bf16[1024,128]{1,0:T(8,128)(2,1)}, bf16[512,1024]{1,0...) async-done(((bf16[1024,512]{1,0:T(8,128)(2,1)}, bf16[1024,128]{1,0:T(8,128)(2,1)}, bf16[1024,128]{1,0:T(8,128)(2,1)}, ...) | async-done | bytes 11272208 | tf_op jit(solution)/shard_map/psum | solution.py:363
  2207.9 129.0 %reduce-scatter.23.cloned.1.call-done = f32[512,1024]{1,0:T(8,128)} async-done(((f32[2048,1024]{1,0:T(8,128)}), f32[512,1024]{1,0:T(8,128)}) %reduce-scatter.23.cloned.1.call-update) | async-done | bytes 2097168 | tf_op jit(solution)/shard_map/reduce_scatter | solution.py:75
  2344.1 33.4 %all-reduce.3 = (f32[1024]{0:T(1024)}, f32[1024]{0:T(1024)}) all-reduce(f32[1024]{0:T(1024)S(1)} %get-tuple-element.333, f32[1024]{0:T(1024)S(1)} %copy-done.33), channel_id=1, replica_groups=mesh['dp'=4,'row'=4,'col'=2] {'dp','row'}, use_global_device_ids=true, to_apply=%region_33.34 | all-reduce | flops 2048 | bytes 16384 | tf_op jit(solution)/shard_map/psum | solution.py:361
  (277 shorter events, 393.1 us)
Async XLA Ops:
  7.2 894.4 %copy-start = (bf16[1408,1024]{1,0:T(8,128)(2,1)S(1)}, bf16[1408,1024]{1,0:T(8,128)(2,1)}, u32[]{:S(2)}) copy-start(bf16[1408,1024]{1,0:T(8,128)(2,1)} %param.33) | copy-start | bytes 8650756
  7.2 94.0 %all-gather.11.cloned.1.call-start = ((), (), s32[]{:S(2)}) async-start(), calls=%async_computation.8 | async-start | bytes 5242880 | tf_op jit(solution)/shard_map/all_gather | solution.py:61
  18.5 142.9 %all-gather.27.cloned.1.call-start = ((), (), s32[]{:S(2)}) async-start(), calls=%async_computation.25 | async-start | bytes 6291456 | tf_op jit(solution)/shard_map/all_gather | solution.py:128
  106.0 112.6 %reduce-scatter.9.cloned.1.call-start = ((), (), s32[]{:S(2)}) async-start(), calls=%async_computation.9 | async-start | bytes 6291456 | tf_op jit(solution)/shard_map/reduce_scatter | solution.py:69
  112.9 187.4 %all-gather.13.cloned.1.call-start = ((), (), s32[]{:S(2)}) async-start(), calls=%async_computation.10 | async-start | bytes 3145728 | tf_op jit(solution)/shard_map/all_gather | solution.py:65
  267.0 185.4 %reduce-scatter.11.cloned.1.call-start = ((), (), s32[]{:S(2)}) async-start(), calls=%async_computation.11 | async-start | bytes 10485760 | tf_op jit(solution)/shard_map/reduce_scatter | solution.py:75
  307.8 153.1 %copy-start.27 = (f32[1024]{0:T(1024)S(1)}, f32[1024]{0:T(1024)}, u32[]{:S(2)}) copy-start(f32[1024]{0:T(1024)} %param.30) | copy-start | bytes 12292
  307.8 237.6 %all-gather.15.cloned.1.call-start = ((), (), s32[]{:S(2)}) async-start(), calls=%async_computation.12 | async-start | bytes 5242880 | tf_op jit(solution)/shard_map/all_gather | solution.py:61
  463.8 356.9 %reduce-scatter.13.cloned.1.call-start = ((), (), s32[]{:S(2)}) async-start(), calls=%async_computation.13 | async-start | bytes 34603008 | tf_op jit(solution)/shard_map/reduce_scatter | solution.py:69
  565.2 336.4 %all-gather.17.cloned.1.call-start = ((), (), s32[]{:S(2)}) async-start(), calls=%async_computation.14 | async-start | bytes 8650752 | tf_op jit(solution)/shard_map/all_gather | solution.py:65
  827.0 229.9 %reduce-scatter.15.cloned.1.call-start = ((), (), s32[]{:S(2)}) async-start(), calls=%async_computation.15 | async-start | bytes 10485760 | tf_op jit(solution)/shard_map/reduce_scatter | solution.py:75
  912.3 276.0 %all-gather.19.cloned.1.call-start = ((), (), s32[]{:S(2)}) async-start(), calls=%async_computation.16 | async-start | bytes 5242880 | tf_op jit(solution)/shard_map/all_gather | solution.py:61
  1107.5 223.9 %reduce-scatter.17.cloned.1.call-start = ((), (), s32[]{:S(2)}) async-start(), calls=%async_computation.17 | async-start | bytes 17301504 | tf_op jit(solution)/shard_map/reduce_scatter | solution.py:69
  1199.5 283.3 %all-gather.21.cloned.1.call-start = ((), (), s32[]{:S(2)}) async-start(), calls=%async_computation.18 | async-start | bytes 17301504 | tf_op jit(solution)/shard_map/all_gather | solution.py:65
  1341.7 303.8 %reduce-scatter.19.cloned.1.call-start = ((), (), s32[]{:S(2)}) async-start(), calls=%async_computation.19 | async-start | bytes 10485760 | tf_op jit(solution)/shard_map/reduce_scatter | solution.py:75
  1500.9 144.6 %copy-start.5 = (f32[512,1024]{1,0:T(8,128)S(1)}, f32[512,1024]{1,0:T(8,128)}, u32[]{:S(2)}) copy-start(f32[512,1024]{1,0:T(8,128)} %get-tuple-element.399) | copy-start | bytes 6291460
  1500.9 239.5 %all-gather.23.cloned.1.call-start = ((), (), s32[]{:S(2)}) async-start(), calls=%async_computation.20 | async-start | bytes 5242880 | tf_op jit(solution)/shard_map/all_gather | solution.py:61
  1658.7 141.6 %reduce-scatter.21.cloned.1.call-start = ((), (), s32[]{:S(2)}) async-start(), calls=%async_computation.21 | async-start | bytes 6291456 | tf_op jit(solution)/shard_map/reduce_scatter | solution.py:69
  1747.3 199.1 %all-reduce.8.cloned.1.call-start = ((), (), s32[]{:S(2)}) async-start(), calls=%async_computation.23 | async-start | bytes 2097152 | tf_op jit(solution)/shard_map/psum | solution.py:309
  1906.3 75.4 %all-gather.25.cloned.1.call-start = ((), (), s32[]{:S(2)}) async-start(), calls=%async_computation.22 | async-start | bytes 3145728 | tf_op jit(solution)/shard_map/all_gather | solution.py:65
  1928.1 261.6 %all-reduce.10.cloned.1.call-start = ((), (), s32[]{:S(2)}) async-start(), calls=%async_computation.26 | async-start | bytes 22544384 | tf_op jit(solution)/shard_map/psum | solution.py:363
  1987.9 348.9 %reduce-scatter.23.cloned.1.call-start = ((), (), s32[]{:S(2)}) async-start(), calls=%async_computation.24 | async-start | bytes 10485760 | tf_op jit(solution)/shard_map/reduce_scatter | solution.py:75
  2207.9 136.2 %copy-start.33 = (f32[1024]{0:T(1024)S(1)}, f32[1024]{0:T(1024)}, u32[]{:S(2)}) copy-start(f32[1024]{0:T(1024)} %get-tuple-element.331) | copy-start | bytes 12292
  2207.9 169.6 %copy-start.35 = (f32[512]{0:T(512)S(1)}, f32[512]{0:T(512)}, u32[]{:S(2)}) copy-start(f32[512]{0:T(512)} %get-tuple-element.424) | copy-start | bytes 6148
  (47 other events, 820.1 us)
Sparse Core Ops, SparseCore 0:
  18.6 82.5 all-gather.10
  106.1 55.2 all-gather.26
  164.3 54.2 reduce-scatter.8
  267.2 33.1 all-gather.12
  307.9 144.4 reduce-scatter.10
  463.9 81.5 all-gather.14
  565.4 255.2 reduce-scatter.12
  827.1 74.4 all-gather.16
  912.4 144.4 reduce-scatter.14
  1107.6 80.7 all-gather.18
  1199.7 131.6 reduce-scatter.16
  1341.8 141.0 all-gather.20
  1501.0 144.4 reduce-scatter.18
  1658.9 81.5 all-gather.22
  1747.4 52.8 reduce-scatter.20
  1906.4 40.0 all-reduce.7
  1948.5 33.1 all-gather.24
  1988.0 201.6 all-reduce.9
  2192.1 144.6 reduce-scatter.22
